TPU v7x, 512 devices: a whole 4x4x16 slice. The times are simulated.
512 devices in a mesh: sector: 16 (over y, x), grp: 32 (over z, core).
Axes of the slice: x: 4, y: 4, z: 16, core: 2. Of those that a mesh axis runs over, the one named last changes fastest.
Arguments:
- start_vector: bfloat16 [8192, 512], P(('sector', 'grp')), may hold values from -130 to 130
- tile_live: int32 [64], P('sector'), may hold values from 32 to 128, as said below
- env_blocks: bfloat16 [64, 384, 128, 128], P('grp', 'sector'), may hold values from -2 to 4
- block_owner: int32 [64, 384, 1], P('grp', 'sector'), may hold values from 0 to 15; in each aligned block of 24 rows (0 to 23, 24 to 47, ..., all dimensions but the last counted through in order) at most 2 rows name the same one
- block_rows: int32 [64, 384], P('grp', 'sector'), may hold values from 0 to 3
- block_cols: int32 [64, 384], P('grp', 'sector'), may hold values from 0 to 3
- site_left: bfloat16 [64, 1024], P('grp'), may hold values from -0.375 to 0.375
- mpo_pattern: int32 [64, 64], P('grp'), may hold values 0 or 1
- site_right: bfloat16 [64, 1024], P('grp'), may hold values from -0.375 to 0.375
- right_env: bfloat16 [64, 1024], P('grp'), may hold values from -0.125 to 0.125
Outputs:
- first_product: bfloat16 [8192, 512], P(('sector', 'grp'))
- second_product: bfloat16 [8192, 512], P(('sector', 'grp'))
Inputs may be any that keep to these rules, and one draw needn't show every extreme that they name: `tile_live`: rows beyond a tile's live count are padding; some tile is full. `block_owner`: in each aligned block of 24 entries of one channel (the blocks one device holds), no owner is named more than 2 times.
All inputs are finite; a program needn't handle non-finite values. No bound on the sum of `mpo_pattern` on one device may be relied on, other than what follows from the above.
Results may differ from a plain program's by a relative error of at most 0.03.
Values may be sent and summed in bfloat16 or wider, within the bound.
A program may use at most 64 MiB of HBM per device.

v0:
```python
import jax
import jax.numpy as jnp
from jax import lax
from jax.sharding import PartitionSpec as P

WM = 64
D1 = 4
RB = 32
TR = 128
TPO = 4
CAP = 2
PHYS = 16
epsilon = 1e-06


def contract(owned_rows, got_blocks, got_codes):
    channels = got_blocks.shape[0]
    slot_count = got_blocks.shape[1] * got_blocks.shape[2]
    results = []
    for channel in range(channels):
        blocks = got_blocks[channel].reshape(slot_count, TR * TR)
        slot_codes = got_codes[channel].reshape(slot_count)
        tile_index = jnp.maximum(slot_codes - 1, 0)
        pair_hot = (
            (tile_index[:, None] == jnp.arange(TPO * TPO, dtype=jnp.int32)[None, :])
            & (slot_codes[:, None] > 0)
        ).astype(jnp.bfloat16)
        summed = jnp.einsum(
            "sp,sq->pq", pair_hot, blocks, preferred_element_type=jnp.float32
        ).astype(jnp.bfloat16)
        dense = summed.reshape(TPO, TPO, TR, TR).transpose(0, 2, 1, 3).reshape(TPO * TR, TPO * TR)
        product = jnp.dot(dense, owned_rows, preferred_element_type=jnp.float32)
        results.append(product.astype(jnp.bfloat16))
    return jnp.stack(results)


def owner_gather(share_rows):
    return lax.all_gather(share_rows, "grp", axis=0, tiled=True)


def channel_share(mixed_rows, mixing):
    return lax.psum_scatter(
        jnp.einsum("wrk,wkn->rn", mixed_rows, mixing, preferred_element_type=jnp.float32).astype(
            jnp.bfloat16
        ),
        "grp",
        scatter_dimension=0,
        tiled=True,
    ).astype(jnp.float32)


def local(
    start_vector,
    tile_live,
    env_blocks,
    block_owner,
    block_rows,
    block_cols,
    site_left,
    mpo_pattern,
    site_right,
    right_env,
):
    sectors = lax.axis_size("sector")
    groups = lax.axis_size("grp")
    share_count = start_vector.shape[0]
    columns = start_vector.shape[1]
    channels = env_blocks.shape[0]
    held_blocks = env_blocks.shape[1]
    right_site, right_panels = (
        lax.all_gather(site_right, "grp", axis=0, tiled=True),
        lax.all_gather(right_env, "grp", axis=0, tiled=True),
    )
    left_site = (
        site_left.reshape(channels, WM, D1, D1) * mpo_pattern.astype(jnp.bfloat16)[:, :, None, None]
    )
    joined = jnp.einsum(
        "wmac,mxbd->wxabcd",
        left_site,
        right_site.reshape(WM, WM, D1, D1),
        preferred_element_type=jnp.float32,
    ).astype(jnp.bfloat16)
    mixing = jnp.einsum(
        "wxq,xr->wqr",
        joined.reshape(channels, WM, PHYS * PHYS),
        right_panels,
        preferred_element_type=jnp.float32,
    ).astype(jnp.bfloat16)
    mixing = (
        mixing.reshape(channels, PHYS, PHYS, RB, RB)
        .transpose(0, 2, 3, 1, 4)
        .reshape(channels, columns, columns)
    )
    owners = block_owner[:, :, 0]
    owner_hot = (owners[:, :, None] == jnp.arange(sectors, dtype=jnp.int32)[None, None, :]).astype(
        jnp.int32
    )
    position = jnp.sum((jnp.cumsum(owner_hot, axis=1) - owner_hot) * owner_hot, axis=2)
    slot_index = owners * CAP + position
    select = slot_index[:, :, None] == jnp.arange(sectors * CAP, dtype=jnp.int32)[None, None, :]
    packed = jnp.einsum(
        "wes,wen->wsn",
        select.astype(jnp.bfloat16),
        env_blocks.reshape(channels, held_blocks, TR * TR),
        preferred_element_type=jnp.float32,
    ).astype(jnp.bfloat16)
    slot_codes = jnp.sum(
        select.astype(jnp.int32) * (1 + block_rows * TPO + block_cols)[:, :, None], axis=1
    )
    got_blocks, got_codes = (
        lax.all_to_all(
            packed.reshape(channels, sectors, CAP, TR * TR),
            "sector",
            split_axis=1,
            concat_axis=1,
            tiled=True,
        ),
        lax.all_to_all(
            slot_codes.reshape(channels, sectors, CAP),
            "sector",
            split_axis=1,
            concat_axis=1,
            tiled=True,
        ),
    )
    tile_mask = (jnp.arange(TR, dtype=jnp.int32)[None, :] < tile_live[:, None]).reshape(TPO * TR)
    owner_mask = tile_mask.astype(jnp.float32)[:, None]
    share_mask = lax.dynamic_slice_in_dim(
        owner_mask, lax.axis_index("grp") * share_count, share_count, 0
    )
    entry_count = float(sectors * groups * share_count * columns)
    owned_rows = owner_gather(start_vector) * owner_mask.astype(jnp.bfloat16)
    first_mixed = contract(owned_rows, got_blocks, got_codes)
    owner_total = lax.psum(
        jnp.einsum("wrk,wkn->rn", first_mixed, mixing, preferred_element_type=jnp.float32).astype(
            jnp.bfloat16
        ),
        "grp",
    ).astype(jnp.float32)
    owner_first = (owner_total * owner_mask).astype(jnp.bfloat16)
    first_product = lax.dynamic_slice_in_dim(
        owner_first, lax.axis_index("grp") * share_count, share_count, 0
    )
    widened = first_product.astype(jnp.float32)
    squares = lax.psum(jnp.sum(widened * widened), ("sector", "grp"))
    inverse_norm = lax.rsqrt(squares / entry_count + epsilon)
    second_mixed = contract(owner_first, got_blocks, got_codes)
    second_product = (channel_share(second_mixed, mixing) * inverse_norm * share_mask).astype(
        jnp.bfloat16
    )
    return (first_product, second_product)


def solution(mesh):
    in_specs = (
        P(("sector", "grp"), None),
        P("sector"),
        P("grp", "sector", None, None),
        P("grp", "sector", None),
        P("grp", "sector"),
        P("grp", "sector"),
        P("grp", None),
        P("grp", None),
        P("grp", None),
        P("grp", None),
    )
    out_specs = (P(("sector", "grp"), None), P(("sector", "grp"), None))
    return jax.shard_map(local, mesh=mesh, in_specs=in_specs, out_specs=out_specs, check_vma=False)
```

profile of v0, /device:TPU:4, one launch (start us, length us, event | category | flops | bytes accessed | tf_op | source)
XLA Modules:
  0.0 513.1 jit_solution(16789400535820442056)
XLA Ops:
  7.2 0.8 fusion.28
  8.0 0.9 select_reduce_fusion.1
  8.8 0.7 fusion.38
  9.5 0.7 add_add_fusion
  10.2 0.1 select_reduce_fusion
  10.4 0.6 copy.24
  11.0 9.1 %all-to-all-start = ((s32[2,16,2]{2,0,1:T(2,128)}), s32[2,16,2]{2,0,1:T(2,128)S(1)}, u32[]{:S(2)}, u32[]{:S(2)}) async-start(s32[2,16,2]{2,0,1:T(2,128)} %copy.24), calls=%async_computation | async-start | bytes 32768 | tf_op jit(solution)/shard_map/all_to_all | solution.py:118
  20.2 3.7 reshape.113
  23.9 2.2 convolution_convert_fusion
  26.1 2.7 reshape.114
  28.8 5.5 %copy.25 = bf16[2,16,2,16384]{3,2,0,1:T(2,128)(2,1)} copy(bf16[2,16,2,16384]{3,2,1,0:T(2,128)(2,1)} %reshape.114) | data formatting | bytes 4194304 | tf_op jit(solution)/shard_map/reshape | solution.py:112
  34.2 7.4 %all-to-all-start.1 = ((bf16[2,16,2,16384]{3,2,0,1:T(2,128)(2,1)}), bf16[2,16,2,16384]{3,2,0,1:T(2,128)(2,1)S(1)}, u32[]{:S(2)}, u32[]{:S(2)}) async-start(bf16[2,16,2,16384]{3,2,0,1:T(2,128)(2,1)} %copy.25), calls=%async_computation.1 | async-start | bytes 4194304 | tf_op jit(solution)/shard_map/all_to_all | solution.py:111
  41.7 34.9 %all-gather = bf16[32,2,1024]{2,1,0:T(2,128)(2,1)S(1)} all-gather(bf16[1,2,1024]{2,1,0:T(2,128)(2,1)S(1)} %bitcast.91), channel_id=1, replica_groups=mesh['sector'=16,'grp'=32] {'grp'}, dimensions={0}, use_global_device_ids=true | all-gather | bytes 135168 | tf_op jit(solution)/shard_map/all_gather | solution.py:71
  76.6 10.0 %reshape.119 = bf16[64,64,4,4]{3,2,1,0:T(4,128)(2,1)} reshape(bf16[32,2,1024]{2,1,0:T(2,128)(2,1)S(1)} %all-gather) | data formatting | bytes 262144 | tf_op jit(solution)/shard_map/reshape | solution.py:80
  86.6 6.4 %copy.34 = bf16[64,64,4,4,1,1]{1,0,3,2,5,4:T(8,128)(2,1)S(1)} copy(bf16[64,64,4,4,1,1]{3,2,1,0,5,4:T(4,128)(2,1)} %bitcast.79) | data formatting | bytes 262144 | tf_op jit(solution)/shard_map/reshape | solution.py:80
  93.0 0.2 mul.83
  93.2 0.2 mul.84
  93.4 0.3 mul.86
  93.7 0.3 fusion.8
  94.1 27.6 %all-gather.1 = bf16[32,2,1024]{2,1,0:T(2,128)(2,1)S(1)} all-gather(bf16[1,2,1024]{2,1,0:T(2,128)(2,1)S(1)} %bitcast.92), channel_id=1, replica_groups=mesh['sector'=16,'grp'=32] {'grp'}, dimensions={0}, use_global_device_ids=true | all-gather | bytes 135168 | tf_op jit(solution)/shard_map/all_gather | solution.py:72
  121.8 0.4 convolution_convert_fusion.3
  122.2 4.3 reshape.121
  126.6 9.0 %copy.32 = bf16[2,16,32,16,32]{4,3,2,1,0:T(8,128)(2,1)} copy(bf16[2,16,32,16,32]{4,2,1,3,0:T(8,128)(2,1)} %bitcast.78) | data formatting | bytes 2097152 | tf_op jit(solution)/shard_map/transpose | solution.py:91
  135.5 6.8 %reshape.122 = bf16[2,512,512]{2,1,0:T(8,128)(2,1)} reshape(bf16[2,16,32,16,32]{4,3,2,1,0:T(8,128)(2,1)} %copy.32) | data formatting | bytes 2097152 | tf_op jit(solution)/shard_map/reshape | solution.py:92
  142.4 32.7 %all_gather.9 = bf16[512,512]{1,0:T(8,128)(2,1)} all-gather(bf16[16,512]{1,0:T(8,128)(2,1)S(1)} %copy-done.2), channel_id=1, replica_groups=mesh['sector'=16,'grp'=32] {'grp'}, dimensions={0}, use_global_device_ids=true | all-gather | bytes 540672 | tf_op jit(solution)/shard_map/all_gather | solution.py:38
  175.3 0.1 gt.27
  175.5 0.1 gt.25
  175.6 2.4 fusion.42
  178.0 1.5 reshape_squeeze.5
  179.5 0.4 fusion.7
  179.9 0.1 copy.42
  180.0 0.4 copy.27
  180.4 0.4 reshape_squeeze.4
  180.9 0.4 fusion.6
  181.4 0.4 copy.26
  181.9 0.5 fusion.3
  182.5 0.5 fusion.2
  183.0 0.1 copy-done
  183.1 1.5 fusion
  184.7 206.9 %all-reduce.2.cloned.1.call-done = bf16[512,512]{1,0:T(8,128)(2,1)} async-done(((bf16[512,512]{1,0:T(8,128)(2,1)}), bf16[512,512]{1,0:T(8,128)(2,1)}) %all-reduce.2.cloned.1.call-update) | async-done | bytes 524304 | tf_op jit(solution)/shard_map/psum | solution.py:134
  391.6 1.2 multiply_convert_fusion
  392.8 0.4 fusion.5
  393.3 0.4 fusion.4
  393.7 1.5 fusion.1
  395.3 1.2 multiply_reduce_fusion
  396.5 104.5 %psum.15 = f32[]{:T(128)} all-reduce(f32[]{:T(128)} %get-tuple-element.6), channel_id=1, replica_groups=mesh['sector'=16,'grp'=32] {'sector','grp'}, use_global_device_ids=true, to_apply=%region_6.7 | all-reduce | flops 1 | bytes 8 | tf_op jit(solution)/shard_map/psum | solution.py:145
  501.7 3.2 reduce-scatter.2.cloned.1.call-done
  504.9 1.4 multiply_convert_fusion.1
  (34 shorter events, 1.0 us)
Async XLA Ops:
  11.0 23.2 %all-to-all-start = ((s32[2,16,2]{2,0,1:T(2,128)}), s32[2,16,2]{2,0,1:T(2,128)S(1)}, u32[]{:S(2)}, u32[]{:S(2)}) async-start(s32[2,16,2]{2,0,1:T(2,128)} %copy.24), calls=%async_computation | async-start | bytes 32768 | tf_op jit(solution)/shard_map/all_to_all | solution.py:118
  34.2 7.5 %copy-start.3 = (bf16[2,1024]{1,0:T(2,128)(2,1)S(1)}, bf16[2,1024]{1,0:T(2,128)(2,1)}, u32[]{:S(2)}) copy-start(bf16[2,1024]{1,0:T(2,128)(2,1)} %param.18) | copy-start | bytes 12292
  34.2 141.4 %all-to-all-start.1 = ((bf16[2,16,2,16384]{3,2,0,1:T(2,128)(2,1)}), bf16[2,16,2,16384]{3,2,0,1:T(2,128)(2,1)S(1)}, u32[]{:S(2)}, u32[]{:S(2)}) async-start(bf16[2,16,2,16384]{3,2,0,1:T(2,128)(2,1)} %copy.25), calls=%async_computation.1 | async-start | bytes 4194304 | tf_op jit(solution)/shard_map/all_to_all | solution.py:111
  41.7 349.9 %all-reduce.2.cloned.1.call-start = ((), (), s32[]{:S(2)}) async-start(), calls=%async_computation.3 | async-start | bytes 1048576 | tf_op jit(solution)/shard_map/psum | solution.py:134
  86.5 6.5 %copy-start.7 = (s32[2,64]{1,0:T(2,128)S(1)}, s32[2,64]{1,0:T(2,128)}, u32[]{:S(2)}) copy-start(s32[2,64]{1,0:T(2,128)} %param.17) | copy-start | bytes 1540
  86.6 6.9 %copy-start.4 = (bf16[2,1024]{1,0:T(2,128)(2,1)S(1)}, bf16[2,1024]{1,0:T(2,128)(2,1)}, u32[]{:S(2)}) copy-start(bf16[2,1024]{1,0:T(2,128)(2,1)} %param.16) | copy-start | bytes 12292
  86.6 7.5 %copy-start.5 = (bf16[2,1024]{1,0:T(2,128)(2,1)S(1)}, bf16[2,1024]{1,0:T(2,128)(2,1)}, u32[]{:S(2)}) copy-start(bf16[2,1024]{1,0:T(2,128)(2,1)} %param.19) | copy-start | bytes 12292
  135.5 6.8 %copy-start.6 = (s32[4]{0:T(128)S(1)}, s32[4]{0:T(128)}, u32[]{:S(2)}) copy-start(s32[4]{0:T(128)} %param.11) | copy-start | bytes 52
  135.5 6.9 %copy-start.2 = (bf16[16,512]{1,0:T(8,128)(2,1)S(1)}, bf16[16,512]{1,0:T(8,128)(2,1)}, u32[]{:S(2)}) copy-start(bf16[16,512]{1,0:T(8,128)(2,1)} %param.10) | copy-start | bytes 49156
  180.9 1.0 copy-start.1
  181.8 1.2 copy-start
  184.6 320.2 %reduce-scatter.2.cloned.1.call-start = ((), (), s32[]{:S(2)}) async-start(), calls=%async_computation.4 | async-start | bytes 540672 | tf_op jit(solution)/shard_map/reduce_scatter | solution.py:42
Sparse Core Ops, SparseCore 0:
  184.8 206.7 all-reduce.1
  395.3 109.4 reduce-scatter.1
where the time goes:
time: 514 us; the launch traced here: 513 us
  waiting for transfers between devices  210 us (41%)
  blocking collectives  200 us (39%)
  local copies, waits for them, and re-layouts  55.9 us (11%)
  starting transfers between devices  16.6 us (3%)
  between operations  15 us (3%)
  matrix products  8.67 us (2%)
  other arithmetic  7.16 us (1%)
    psum x1, waiting for transfers between devices, local(): lax.psum(jnp.einsum('wrk,wkn->rn', first_mixed, mixing, preferred_element...  207 us
    psum x1, blocking collectives, local(): squares = lax.psum(jnp.sum(widened * widened), ('sector', 'grp'))  105 us
    all_gather x1, blocking collectives, local(): lax.all_gather(site_right, 'grp', axis=0, tiled=True)  34.9 us
    all_gather x1, blocking collectives, owner_gather(): return lax.all_gather(share_rows, 'grp', axis=0, tiled=True)  32.7 us
    all_gather x1, blocking collectives, local(): lax.all_gather(right_env, 'grp', axis=0, tiled=True)  27.6 us
    reshape x2, local copies, waits for them, and re-layouts, local(): right_site.reshape(WM, WM, D1, D1)  16.4 us
  transfers between devices with their start and end apart: 4, of which 2 were waited for; matrix products, arithmetic and copies ran while one was open for 11% of the time, Pallas kernels for 0%

commit v1 on v0

--- a/solution.py
+++ b/solution.py
@@ -131,11 +131,14 @@
     entry_count = float(sectors * groups * share_count * columns)
     owned_rows = owner_gather(start_vector) * owner_mask.astype(jnp.bfloat16)
     first_mixed = contract(owned_rows, got_blocks, got_codes)
-    owner_total = lax.psum(
-        jnp.einsum("wrk,wkn->rn", first_mixed, mixing, preferred_element_type=jnp.float32).astype(
-            jnp.bfloat16
+    owner_total = jnp.sum(
+        lax.all_gather(
+            jnp.einsum(
+                "wrk,wkn->rn", first_mixed, mixing, preferred_element_type=jnp.float32
+            ).astype(jnp.bfloat16),
+            "grp",
         ),
-        "grp",
+        axis=0,
     ).astype(jnp.float32)
     owner_first = (owner_total * owner_mask).astype(jnp.bfloat16)
     first_product = lax.dynamic_slice_in_dim(

time: 514 us -> 416 us (0.81)
  the two profiles are of different devices: /device:TPU:4 before, /device:TPU:2 now
where the time goes in v1:
time: 416 us; the launch traced here: 415 us
  blocking collectives  197 us (47%)
  waiting for transfers between devices  107 us (26%)
  local copies, waits for them, and re-layouts  55.9 us (13%)
  starting transfers between devices  16.7 us (4%)
  other arithmetic  15 us (4%)
  between operations  15 us (4%)
  matrix products  8.66 us (2%)
    all_gather x1, waiting for transfers between devices, local(): lax.all_gather(jnp.einsum('wrk,wkn->rn', first_mixed, mixing, preferred_e...  103 us
    psum x1, blocking collectives, local(): squares = lax.psum(jnp.sum(widened * widened), ('sector', 'grp'))  102 us
    all_gather x1, blocking collectives, local(): lax.all_gather(site_right, 'grp', axis=0, tiled=True)  34.9 us
    all_gather x1, blocking collectives, owner_gather(): return lax.all_gather(share_rows, 'grp', axis=0, tiled=True)  32.7 us
    all_gather x1, blocking collectives, local(): lax.all_gather(right_env, 'grp', axis=0, tiled=True)  27.6 us
    reshape x2, local copies, waits for them, and re-layouts, local(): right_site.reshape(WM, WM, D1, D1)  16.4 us
    all_to_all x1, starting transfers between devices, local(): lax.all_to_all(slot_codes.reshape(channels, sectors, CAP), 'sector', spli...  9.16 us
    transpose x1, local copies, waits for them, and re-layouts, local(): mixing = mixing.reshape(channels, PHYS, PHYS, RB, RB).transpose(0, 2, 3,...  8.97 us
  transfers between devices with their start and end apart: 4, of which 2 were waited for; matrix products, arithmetic and copies ran while one was open for 13% of the time, Pallas kernels for 0%

profile of v1, /device:TPU:2, one launch (start us, length us, event | category | flops | bytes accessed | tf_op | source)
XLA Modules:
  0.0 414.7 jit_solution(12863901055881200200)
XLA Ops:
  7.2 0.8 fusion.28
  8.0 0.9 select_reduce_fusion.1
  8.8 0.7 fusion.38
  9.5 0.7 add_add_fusion
  10.2 0.1 select_reduce_fusion
  10.4 0.6 copy.24
  11.0 9.2 %all-to-all-start = ((s32[2,16,2]{2,0,1:T(2,128)}), s32[2,16,2]{2,0,1:T(2,128)S(1)}, u32[]{:S(2)}, u32[]{:S(2)}) async-start(s32[2,16,2]{2,0,1:T(2,128)} %copy.24), calls=%async_computation | async-start | bytes 32768 | tf_op jit(solution)/shard_map/all_to_all | solution.py:118
  20.2 3.7 reshape.113
  23.9 2.2 convolution_convert_fusion
  26.1 2.7 reshape.114
  28.8 5.5 %copy.25 = bf16[2,16,2,16384]{3,2,0,1:T(2,128)(2,1)} copy(bf16[2,16,2,16384]{3,2,1,0:T(2,128)(2,1)} %reshape.114) | data formatting | bytes 4194304 | tf_op jit(solution)/shard_map/reshape | solution.py:112
  34.3 7.4 %all-to-all-start.1 = ((bf16[2,16,2,16384]{3,2,0,1:T(2,128)(2,1)}), bf16[2,16,2,16384]{3,2,0,1:T(2,128)(2,1)S(1)}, u32[]{:S(2)}, u32[]{:S(2)}) async-start(bf16[2,16,2,16384]{3,2,0,1:T(2,128)(2,1)} %copy.25), calls=%async_computation.1 | async-start | bytes 4194304 | tf_op jit(solution)/shard_map/all_to_all | solution.py:111
  41.7 34.9 %all-gather.1 = bf16[32,2,1024]{2,1,0:T(2,128)(2,1)S(1)} all-gather(bf16[1,2,1024]{2,1,0:T(2,128)(2,1)S(1)} %bitcast.93), channel_id=1, replica_groups=mesh['sector'=16,'grp'=32] {'grp'}, dimensions={0}, use_global_device_ids=true | all-gather | bytes 135168 | tf_op jit(solution)/shard_map/all_gather | solution.py:71
  76.6 10.0 %reshape.119 = bf16[64,64,4,4]{3,2,1,0:T(4,128)(2,1)} reshape(bf16[32,2,1024]{2,1,0:T(2,128)(2,1)S(1)} %all-gather.1) | data formatting | bytes 262144 | tf_op jit(solution)/shard_map/reshape | solution.py:80
  86.6 6.4 %copy.34 = bf16[64,64,4,4,1,1]{1,0,3,2,5,4:T(8,128)(2,1)S(1)} copy(bf16[64,64,4,4,1,1]{3,2,1,0,5,4:T(4,128)(2,1)} %bitcast.81) | data formatting | bytes 262144 | tf_op jit(solution)/shard_map/reshape | solution.py:80
  93.1 0.2 mul.83
  93.3 0.2 mul.84
  93.5 0.3 mul.86
  93.8 0.3 fusion.8
  94.1 27.6 %all-gather.2 = bf16[32,2,1024]{2,1,0:T(2,128)(2,1)S(1)} all-gather(bf16[1,2,1024]{2,1,0:T(2,128)(2,1)S(1)} %bitcast.94), channel_id=1, replica_groups=mesh['sector'=16,'grp'=32] {'grp'}, dimensions={0}, use_global_device_ids=true | all-gather | bytes 135168 | tf_op jit(solution)/shard_map/all_gather | solution.py:72
  121.8 0.4 convolution_convert_fusion.3
  122.2 4.3 %reshape.121 = bf16[2,16,16,32,32]{4,3,2,1,0:T(8,128)(2,1)} reshape(bf16[2,256,1024]{2,1,0:T(8,128)(2,1)S(1)} %convolution_convert_fusion.3) | data formatting | bytes 2097152 | tf_op jit(solution)/shard_map/reshape | solution.py:90
  126.6 9.0 %copy.32 = bf16[2,16,32,16,32]{4,3,2,1,0:T(8,128)(2,1)} copy(bf16[2,16,32,16,32]{4,2,1,3,0:T(8,128)(2,1)} %bitcast.80) | data formatting | bytes 2097152 | tf_op jit(solution)/shard_map/transpose | solution.py:91
  135.6 6.8 %reshape.122 = bf16[2,512,512]{2,1,0:T(8,128)(2,1)} reshape(bf16[2,16,32,16,32]{4,3,2,1,0:T(8,128)(2,1)} %copy.32) | data formatting | bytes 2097152 | tf_op jit(solution)/shard_map/reshape | solution.py:92
  142.5 32.7 %all_gather.15 = bf16[512,512]{1,0:T(8,128)(2,1)} all-gather(bf16[16,512]{1,0:T(8,128)(2,1)S(1)} %copy-done.4), channel_id=1, replica_groups=mesh['sector'=16,'grp'=32] {'grp'}, dimensions={0}, use_global_device_ids=true | all-gather | bytes 540672 | tf_op jit(solution)/shard_map/all_gather | solution.py:38
  175.4 0.1 gt.25
  175.6 0.1 gt.27
  175.7 2.4 fusion.42
  178.1 1.5 reshape_squeeze.4
  179.5 0.4 fusion.6
  180.1 0.4 copy.26
  180.5 0.4 reshape_squeeze.5
  180.9 0.4 fusion.7
  181.5 0.4 copy.27
  182.0 0.5 fusion.2
  182.5 0.5 fusion.3
  183.0 0.1 copy-done
  183.1 1.5 fusion
  184.7 102.6 %all-gather.5.cloned.1.call-done = bf16[16384,512]{1,0:T(8,128)(2,1)} async-done(((bf16[512,512]{1,0:T(8,128)(2,1)}), bf16[16384,512]{1,0:T(8,128)(2,1)}) %all-gather.5.cloned.1.call-update) | async-done | bytes 16777232 | tf_op jit(solution)/shard_map/all_gather | solution.py:135
  287.3 8.8 %reduce_sum.44 = bf16[512,512]{1,0:T(8,128)(2,1)S(1)} reduce(bf16[32,512,512]{2,1,0:T(8,128)(2,1)} %bitcast.79, bf16[]{:T(256)} %constant.11.clone.1), dimensions={0}, to_apply=%region_3.4 | reduce | flops 8126464 | bytes 17301506 | tf_op jit(solution)/shard_map/reduce_sum | solution.py:134
  296.1 0.2 multiply_convert_fusion
  296.3 0.4 fusion.4
  296.8 0.4 fusion.5
  297.2 1.5 fusion.1
  298.8 1.2 multiply_reduce_fusion
  300.0 101.8 %psum.7 = f32[]{:T(128)} all-reduce(f32[]{:T(128)} %get-tuple-element.6), channel_id=1, replica_groups=mesh['sector'=16,'grp'=32] {'sector','grp'}, use_global_device_ids=true, to_apply=%region_6.7 | all-reduce | flops 1 | bytes 8 | tf_op jit(solution)/shard_map/psum | solution.py:148
  402.5 4.0 reduce-scatter.2.cloned.1.call-done
  406.5 1.4 multiply_convert_fusion.1
  (39 shorter events, 1.1 us)
Async XLA Ops:
  11.0 23.2 %all-to-all-start = ((s32[2,16,2]{2,0,1:T(2,128)}), s32[2,16,2]{2,0,1:T(2,128)S(1)}, u32[]{:S(2)}, u32[]{:S(2)}) async-start(s32[2,16,2]{2,0,1:T(2,128)} %copy.24), calls=%async_computation | async-start | bytes 32768 | tf_op jit(solution)/shard_map/all_to_all | solution.py:118
  34.3 7.5 %copy-start.5 = (bf16[2,1024]{1,0:T(2,128)(2,1)S(1)}, bf16[2,1024]{1,0:T(2,128)(2,1)}, u32[]{:S(2)}) copy-start(bf16[2,1024]{1,0:T(2,128)(2,1)} %param.18) | copy-start | bytes 12292
  34.3 141.4 %all-to-all-start.1 = ((bf16[2,16,2,16384]{3,2,0,1:T(2,128)(2,1)}), bf16[2,16,2,16384]{3,2,0,1:T(2,128)(2,1)S(1)}, u32[]{:S(2)}, u32[]{:S(2)}) async-start(bf16[2,16,2,16384]{3,2,0,1:T(2,128)(2,1)} %copy.25), calls=%async_computation.1 | async-start | bytes 4194304 | tf_op jit(solution)/shard_map/all_to_all | solution.py:111
  41.7 245.6 %all-gather.5.cloned.1.call-start = ((), (), s32[]{:S(2)}) async-start(), calls=%async_computation.4 | async-start | bytes 17301504 | tf_op jit(solution)/shard_map/all_gather | solution.py:135
  86.6 6.5 %copy-start.9 = (s32[2,64]{1,0:T(2,128)S(1)}, s32[2,64]{1,0:T(2,128)}, u32[]{:S(2)}) copy-start(s32[2,64]{1,0:T(2,128)} %param.17) | copy-start | bytes 1540
  86.6 6.9 %copy-start.6 = (bf16[2,1024]{1,0:T(2,128)(2,1)S(1)}, bf16[2,1024]{1,0:T(2,128)(2,1)}, u32[]{:S(2)}) copy-start(bf16[2,1024]{1,0:T(2,128)(2,1)} %param.16) | copy-start | bytes 12292
  86.6 7.5 %copy-start.7 = (bf16[2,1024]{1,0:T(2,128)(2,1)S(1)}, bf16[2,1024]{1,0:T(2,128)(2,1)}, u32[]{:S(2)}) copy-start(bf16[2,1024]{1,0:T(2,128)(2,1)} %param.19) | copy-start | bytes 12292
  135.6 6.8 %copy-start.8 = (s32[4]{0:T(128)S(1)}, s32[4]{0:T(128)}, u32[]{:S(2)}) copy-start(s32[4]{0:T(128)} %param.11) | copy-start | bytes 52
  135.6 6.9 %copy-start.4 = (bf16[16,512]{1,0:T(8,128)(2,1)S(1)}, bf16[16,512]{1,0:T(8,128)(2,1)}, u32[]{:S(2)}) copy-start(bf16[16,512]{1,0:T(8,128)(2,1)} %param.10) | copy-start | bytes 49156
  180.5 1.4 copy-start.2
  180.9 1.0 copy-start.1
  181.9 1.2 copy-start
  184.7 221.8 %reduce-scatter.2.cloned.1.call-start = ((), (), s32[]{:S(2)}) async-start(), calls=%async_computation.3 | async-start | bytes 540672 | tf_op jit(solution)/shard_map/reduce_scatter | solution.py:42
  287.3 9.0 %copy-start.3 = (bf16[4,4,128,128]{3,1,2,0:T(4,128)(2,1)S(1)}, bf16[4,4,128,128]{3,1,2,0:T(4,128)(2,1)}, u32[]{:S(2)}) copy-start(bf16[4,4,128,128]{3,1,2,0:T(4,128)(2,1)} %copy-done.2) | copy-start | bytes 1572868
Sparse Core Ops, SparseCore 0:
  184.8 102.4 all-gather.4
  298.8 107.6 reduce-scatter.1
